TPU v7x, 32 devices: a whole 2x2x4 slice. The times are simulated.
32 devices in a mesh: role: 4 (over y, x), dom: 8 (over z, core).
Axes of the slice: x: 2, y: 2, z: 4, core: 2. Of those that a mesh axis runs over, the one named last changes fastest.
Arguments:
- node_feats: bfloat16 [4096, 512], P(('role', 'dom')), may hold values from -6 to 6
- hub_feats: bfloat16 [128, 512], P(('role', 'dom')), may hold values from -6 to 6
- weight: bfloat16 [1024, 512], replicated, may hold values from -0.1875 to 0.1875
- edge_src: int32 [32, 1024], P(('role', 'dom')), may hold values from 0 to 287, as said below
- edge_dst: int32 [32, 1024], P(('role', 'dom')), may hold values from 0 to 127, as said below
- bound_rows: int32 [32, 16], P(('role', 'dom')), may hold values from 0 to 127
- hub_edge_src: int32 [32, 128], P(('role', 'dom')), may hold values from 0 to 127
- hub_edge_slot: int32 [32, 128], P(('role', 'dom')), may hold values from 0 to 63, as said below
- slot_hub: int32 [32, 64], P(('role', 'dom')), may hold values from 0 to 3, as said below
Outputs:
- node_out: bfloat16 [4096, 512], P(('role', 'dom'))
- hub_out: bfloat16 [128, 512], P(('role', 'dom'))
Inputs may be any that keep to these rules, and one draw needn't show every extreme that they name: `edge_src`: row indices into the source table of the device: its own nodes, then 16 rows of the device before it along dom, then 16 of the device after it, then the 128 hubs. `edge_dst`: each node of a device is the destination of at least one of the device's edges. `hub_edge_slot`: every slot of a device receives at least one of its hub edges; slot s belongs to the owner numbered s // 2. `slot_hub`: every hub of every owner is fed by at least one slot of some device.
All inputs are finite; a program needn't handle non-finite values.
Results may differ from a plain program's by a relative error of at most 0.0027.
Values may be sent and summed in bfloat16 or wider, within the bound.
A program may use at most 64 MiB of HBM per device.

v0:
```python
import math

import jax
import jax.numpy as jnp
from jax import lax
from jax.sharding import PartitionSpec as P

epsilon = 1e-06


def extended(block, sides, width):
    for axis, dim in sides:
        count = lax.axis_size(axis)
        forward = [(i, i + 1) for i in range(count - 1)]
        forward.append((count - 1, 0))
        backward = [(target, source) for source, target in forward]
        low = lax.ppermute(
            lax.slice_in_dim(block, block.shape[dim] - width, None, axis=dim), axis, forward
        )
        high = lax.ppermute(lax.slice_in_dim(block, 0, width, axis=dim), axis, backward)
        block = jnp.concatenate([low, block, high], axis=dim)
    return block


def sage_update(self_rows, mean_rows, weight):
    feature_width = self_rows.shape[1]
    linear = jnp.dot(self_rows, weight[:feature_width], preferred_element_type=jnp.float32)
    linear = linear + jnp.dot(mean_rows, weight[feature_width:], preferred_element_type=jnp.float32)
    rectified = jnp.maximum(linear, 0.0)
    inverse_norm = lax.rsqrt(jnp.mean(rectified * rectified, axis=1, keepdims=True) + epsilon)
    return (rectified * inverse_norm).astype(jnp.bfloat16)


def on_device(
    node_feats,
    hub_feats,
    weight,
    edge_src,
    edge_dst,
    bound_rows,
    hub_edge_src,
    hub_edge_slot,
    slot_hub,
):
    feature_width = node_feats.shape[1]
    local_nodes = node_feats.shape[0]
    hub_local = hub_feats.shape[0]
    exports = node_feats[bound_rows[0]]
    bound_size = exports.shape[0]
    widened = extended(exports, (("dom", 0),), bound_size)
    hub_table = lax.all_gather(hub_feats, ("role", "dom"), axis=0, tiled=True)
    source_table = jnp.concatenate(
        [node_feats, widened[:bound_size], widened[2 * bound_size :], hub_table], axis=0
    )
    sources = edge_src[0]
    targets = edge_dst[0]
    edge_block = math.gcd(sources.shape[0], 2048)

    def add_block(sums, indices):
        node_sums, node_degree = sums
        block_sources, block_targets = indices
        picked = source_table[block_sources].astype(jnp.float32)
        return (
            (node_sums.at[block_targets].add(picked), node_degree.at[block_targets].add(1.0)),
            None,
        )

    initial = (
        jnp.zeros((local_nodes, feature_width), jnp.float32),
        jnp.zeros((local_nodes,), jnp.float32),
    )
    (node_sums, node_degree), unused = lax.scan(
        add_block, initial, (sources.reshape(-1, edge_block), targets.reshape(-1, edge_block))
    )
    hub_sources = hub_edge_src[0]
    hub_slots = hub_edge_slot[0]
    slot_table = slot_hub[0]
    slot_total = slot_table.shape[0]
    role_count = lax.axis_size("role")
    dom_count = lax.axis_size("dom")
    per_owner = slot_total // (role_count * dom_count)
    partial_value = (
        jnp.zeros((slot_total, feature_width), jnp.float32)
        .at[hub_slots]
        .add(node_feats[hub_sources].astype(jnp.float32))
    )
    slot_counts = jnp.zeros((slot_total,), jnp.float32).at[hub_slots].add(1.0)
    outgoing = (
        partial_value.reshape(role_count, dom_count, per_owner, feature_width),
        slot_counts.reshape(role_count, dom_count, per_owner),
        slot_table.astype(jnp.float32).reshape(role_count, dom_count, per_owner),
    )
    incoming_rows, incoming_counts, incoming_hubs = (
        lax.all_to_all(
            lax.all_to_all(outgoing[0], "role", split_axis=0, concat_axis=0, tiled=True),
            "dom",
            split_axis=1,
            concat_axis=1,
            tiled=True,
        ),
        lax.all_to_all(
            lax.all_to_all(outgoing[1], "role", split_axis=0, concat_axis=0, tiled=True),
            "dom",
            split_axis=1,
            concat_axis=1,
            tiled=True,
        ),
        lax.all_to_all(
            lax.all_to_all(outgoing[2], "role", split_axis=0, concat_axis=0, tiled=True),
            "dom",
            split_axis=1,
            concat_axis=1,
            tiled=True,
        ),
    )
    incoming_rows = incoming_rows.reshape(-1, feature_width)
    onehot = (
        incoming_hubs.reshape(-1)[:, None] == jnp.arange(hub_local, dtype=jnp.float32)[None, :]
    ).astype(jnp.float32)
    hub_sums = jnp.dot(
        onehot.T, incoming_rows, precision=lax.Precision.HIGHEST, preferred_element_type=jnp.float32
    )
    hub_degree = jnp.dot(
        incoming_counts.reshape(-1),
        onehot,
        precision=lax.Precision.HIGHEST,
        preferred_element_type=jnp.float32,
    )
    node_mean = (node_sums / node_degree[:, None]).astype(jnp.bfloat16)
    node_out = sage_update(node_feats, node_mean, weight)
    hub_mean = (hub_sums / hub_degree[:, None]).astype(jnp.bfloat16)
    hub_out = sage_update(hub_feats, hub_mean, weight)
    return (node_out, hub_out)


def solution(mesh):
    return jax.shard_map(
        on_device,
        mesh=mesh,
        in_specs=(
            P(("role", "dom"), None),
            P(("role", "dom"), None),
            P(),
            P(("role", "dom"), None),
            P(("role", "dom"), None),
            P(("role", "dom"), None),
            P(("role", "dom"), None),
            P(("role", "dom"), None),
            P(("role", "dom"), None),
        ),
        out_specs=(P(("role", "dom"), None), P(("role", "dom"), None)),
        check_vma=False,
    )
```

profile of v0, /device:TPU:0, one launch (start us, length us, event | category | flops | bytes accessed | tf_op | source)
XLA Modules:
  0.0 118.5 jit_solution(10749074931665273671)
XLA Ops:
  0.6 0.0 copy-start
  0.6 0.0 copy-start.1
  0.7 0.0 copy-start.2
  0.7 0.0 copy-start.3
  0.7 0.0 copy-start.4
  0.7 0.0 copy-start.5
  0.7 0.0 copy-start.6
  0.7 0.7 fusion.18
  1.5 1.5 %gather_fusion = bf16[16,512]{1,0:T(8,128)(2,1)S(1)} fusion(bf16[128,512]{1,0:T(8,128)(2,1)} %param.9, s32[1024]{0:T(1024)S(1)} %pad_clamp_fusion.1), kind=kCustom, calls=%fused_computation | custom fusion | bytes 32832 | tf_op jit(solution)/shard_map/gather | solution.py:48
  3.0 0.5 collective-permute-start
  3.5 4.1 %collective-permute-start.1 = (bf16[16,512]{1,0:T(8,128)(2,1)S(1)}, bf16[16,512]{1,0:T(8,128)(2,1)S(1)}, u32[]{:S(2)}, u32[]{:S(2)}) collective-permute-start(bf16[16,512]{1,0:T(8,128)(2,1)S(1)} %gather_fusion), channel_id=1, source_target_pairs={{1,0},{2,1},{3,2},{4,3},{5,4},{6,5},{7,6},{0,7},{9,8},{10,9},{11,1... | collective-permute-start | bytes 49160 | tf_op jit(solution)/shard_map/ppermute | solution.py:20
  7.6 0.7 fusion.19
  8.3 1.4 %scatter_custom_fusion.3 = f32[64]{0:T(128)S(1)} fusion(s32[128]{0:T(128)S(1)} %fusion.19, f32[128]{0:T(128)S(1)} %broadcast.143, f32[]{:T(128)} %constant.9.clone.1), kind=kCustom, calls=%fused_computation.50 | custom fusion | flops 128 | bytes 260 | tf_op jit(solution)/shard_map/scatter-add | solution.py:87
  9.7 0.1 reshape.180
  9.8 0.7 copy.22
  10.5 4.2 %all-to-all-start.4 = ((f32[4,8,2]{1,2,0:T(2,128)}), f32[4,8,2]{1,2,0:T(2,128)S(1)}, u32[]{:S(2)}, u32[]{:S(2)}) async-start(f32[4,8,2]{1,2,0:T(2,128)} %copy.22), calls=%async_computation.4 | async-start | bytes 8192 | tf_op jit(solution)/shard_map/all_to_all | solution.py:102
  14.6 1.3 %fusion.9 = f32[128,512]{1,0:T(8,128)S(1)} fusion(bf16[128,512]{1,0:T(8,128)(2,1)} %param.9, bf16[1024,512]{1,0:T(8,128)(2,1)} %param.11), kind=kOutput, calls=%fused_computation.20 | convolution fusion | flops 67108864 | bytes 917504 | tf_op jit(solution)/shard_map/dot_general | solution.py:27
  16.0 0.0 copy-done
  16.0 0.9 fusion.7
  16.9 0.0 copy-done.3
  16.9 0.0 copy-done.4
  16.9 0.0 copy-done.5
  16.9 0.1 convert_element_type.31
  17.1 0.7 copy.17
  17.7 1.6 %all-to-all-done.4 = f32[4,8,2]{1,2,0:T(2,128)S(1)} async-done(((f32[4,8,2]{1,2,0:T(2,128)}), f32[4,8,2]{1,2,0:T(2,128)S(1)}, u32[]{:S(2)}, u32[]{:S(2)}) %all-to-all-start.4) | async-done | bytes 288 | tf_op jit(solution)/shard_map/all_to_all | solution.py:102
  19.3 3.2 %all-to-all-start = ((f32[4,8,2]{1,2,0:T(2,128)}), f32[4,8,2]{1,2,0:T(2,128)S(1)}, u32[]{:S(2)}, u32[]{:S(2)}) async-start(f32[4,8,2]{1,2,0:T(2,128)} %copy.17), calls=%async_computation | async-start | bytes 8192 | tf_op jit(solution)/shard_map/all_to_all | solution.py:109
  22.6 0.0 copy-done.6
  22.6 0.7 copy.23
  23.3 3.9 %all-to-all-done = f32[4,8,2]{1,2,0:T(2,128)S(1)} async-done(((f32[4,8,2]{1,2,0:T(2,128)}), f32[4,8,2]{1,2,0:T(2,128)S(1)}, u32[]{:S(2)}, u32[]{:S(2)}) %all-to-all-start) | async-done | bytes 288 | tf_op jit(solution)/shard_map/all_to_all | solution.py:109
  27.2 3.3 %all-to-all-start.5 = ((f32[4,8,2]{0,2,1:T(2,128)}), f32[4,8,2]{0,2,1:T(2,128)S(1)}, u32[]{:S(2)}, u32[]{:S(2)}) async-start(f32[4,8,2]{0,2,1:T(2,128)} %copy.23), calls=%async_computation.5 | async-start | bytes 16384 | tf_op jit(solution)/shard_map/all_to_all | solution.py:101
  30.6 0.7 copy.18
  31.3 4.8 %all-to-all-done.5 = f32[4,8,2]{0,2,1:T(2,128)S(1)} async-done(((f32[4,8,2]{0,2,1:T(2,128)}), f32[4,8,2]{0,2,1:T(2,128)S(1)}, u32[]{:S(2)}, u32[]{:S(2)}) %all-to-all-start.5) | async-done | bytes 288 | tf_op jit(solution)/shard_map/all_to_all | solution.py:101
  36.1 3.3 %all-to-all-start.1 = ((f32[4,8,2]{0,2,1:T(2,128)}), f32[4,8,2]{0,2,1:T(2,128)S(1)}, u32[]{:S(2)}, u32[]{:S(2)}) async-start(f32[4,8,2]{0,2,1:T(2,128)} %copy.18), calls=%async_computation.1 | async-start | bytes 16384 | tf_op jit(solution)/shard_map/all_to_all | solution.py:108
  39.4 0.0 copy-done.2
  39.4 40.5 %all-gather = bf16[32,4,512]{2,1,0:T(4,128)(2,1)S(1)} all-gather(bf16[1,4,512]{2,1,0:T(4,128)(2,1)S(1)} %bitcast.26), channel_id=1, replica_groups=mesh['role'=4,'dom'=8] {'role','dom'}, dimensions={0}, use_global_device_ids=true | all-gather | bytes 135168 | tf_op jit(solution)/shard_map/all_gather | solution.py:51
  80.0 0.0 copy-done.1
  80.0 2.0 %scatter_custom_fusion.2 = f32[64,512]{1,0:T(8,128)S(1)} fusion(s32[128]{0:T(128)S(1)} %fusion.19, f32[]{:T(128)} %constant.9.clone.1, bf16[128,512]{1,0:T(8,128)(2,1)S(1)} %copy-done.1, s32[1024]{0:T(1024)S(1)} %pad_clamp_fusion), kind=kCustom, calls=%fused_computation.23 | custom fusion | flops 131072 | bytes 266244 | tf_op jit(solution)/shard_map/scatter-add | solution.py:85
  81.9 0.7 reshape.178
  82.7 7.6 %scatter_custom_fusion.1 = f32[128]{0:T(128)S(1)} fusion(s32[1024]{0:T(1024)S(1)} %bitcast.28, f32[1024]{0:T(1024)S(1)} %broadcast.142, f32[]{:T(128)} %constant.9.clone.1), kind=kCustom, calls=%fused_computation.52 | custom fusion | flops 1024 | bytes 516 | tf_op jit(solution)/shard_map/while/body/eval_jaxpr/scatter-add | solution.py:64
  90.3 0.1 copy.24
  90.5 0.1 reshape.240
  90.6 0.0 all-to-all-done.1
  90.6 3.3 %all-to-all-start.2 = ((f32[4,8,2,512]{3,2,1,0:T(2,128)}), f32[4,8,2,512]{3,2,1,0:T(2,128)S(1)}, u32[]{:S(2)}, u32[]{:S(2)}) async-start(f32[4,8,2,512]{3,2,1,0:T(2,128)} %reshape.178), calls=%async_computation.2 | async-start | bytes 262144 | tf_op jit(solution)/shard_map/all_to_all | solution.py:95
  93.9 0.1 copy.19
  94.1 0.1 eq.15
  94.2 0.2 convolution_bitcast_fusion
  94.4 0.0 collective-permute-done
  94.4 0.0 collective-permute-done.1
  94.4 11.6 %scatter_custom_fusion = f32[128,512]{1,0:T(8,128)S(1)} fusion(s32[1024]{0:T(1024)S(1)} %bitcast.29, f32[]{:T(128)} %constant.9.clone.1, bf16[288,512]{1,0:T(8,128)(2,1)S(1)} %pad_maximum_fusion, s32[1024]{0:T(1024)S(1)} %broadcast_clamp_fusion), kind=kCustom, calls=%fused_computation.7 | custom fusion | flops 1048576 | bytes 561156 | tf_op jit(solution)/shard_map/while/body/eval_jaxpr/scatter-add | solution.py:64
  106.0 0.4 multiply_reduce_fusion
  106.4 0.0 all-to-all-done.2
  106.4 0.7 copy.20
  107.0 3.4 %all-to-all-start.3 = ((f32[4,8,2,512]{3,2,0,1:T(2,128)}), f32[4,8,2,512]{3,2,0,1:T(2,128)S(1)}, u32[]{:S(2)}, u32[]{:S(2)}) async-start(f32[4,8,2,512]{3,2,0,1:T(2,128)} %copy.20), calls=%async_computation.3 | async-start | bytes 262144 | tf_op jit(solution)/shard_map/all_to_all | solution.py:94
  110.4 0.7 multiply_convert_fusion
  111.2 5.9 %all-to-all-done.3 = f32[4,8,2,512]{3,2,0,1:T(2,128)S(1)} async-done(((f32[4,8,2,512]{3,2,0,1:T(2,128)}), f32[4,8,2,512]{3,2,0,1:T(2,128)S(1)}, u32[]{:S(2)}, u32[]{:S(2)}) %all-to-all-start.3) | async-done | bytes 131104 | tf_op jit(solution)/shard_map/all_to_all | solution.py:94
  117.1 0.1 reshape.179
  117.2 0.3 fusion.4
  117.5 0.3 multiply_reduce_fusion.1
  117.8 0.7 multiply_convert_fusion.1
  (14 shorter events, 0.2 us)
Async XLA Ops:
  0.6 15.4 %copy-start = (bf16[1024,512]{1,0:T(8,128)(2,1)S(1)}, bf16[1024,512]{1,0:T(8,128)(2,1)}, u32[]{:S(2)}) copy-start(bf16[1024,512]{1,0:T(8,128)(2,1)} %param.11) | copy-start | bytes 3145732
  0.6 79.3 %copy-start.1 = (bf16[128,512]{1,0:T(8,128)(2,1)S(1)}, bf16[128,512]{1,0:T(8,128)(2,1)}, u32[]{:S(2)}) copy-start(bf16[128,512]{1,0:T(8,128)(2,1)} %param.9) | copy-start | bytes 393220
  0.7 38.8 %copy-start.2 = (bf16[4,512]{1,0:T(4,128)(2,1)S(1)}, bf16[4,512]{1,0:T(4,128)(2,1)}, u32[]{:S(2)}) copy-start(bf16[4,512]{1,0:T(4,128)(2,1)} %param.10) | copy-start | bytes 12292
  0.7 16.2 %copy-start.3 = (s32[1,1024]{1,0:T(1,128)S(1)}, s32[1,1024]{1,0:T(1,128)}, u32[]{:S(2)}) copy-start(s32[1,1024]{1,0:T(1,128)} %param.13) | copy-start | bytes 12292
  0.7 16.2 %copy-start.4 = (s32[1,1024]{1,0:T(1,128)S(1)}, s32[1,1024]{1,0:T(1,128)}, u32[]{:S(2)}) copy-start(s32[1,1024]{1,0:T(1,128)} %param.12) | copy-start | bytes 12292
  0.7 16.2 %copy-start.5 = (s32[1,64]{1,0:T(1,128)S(1)}, s32[1,64]{1,0:T(1,128)}, u32[]{:S(2)}) copy-start(s32[1,64]{1,0:T(1,128)} %param.17) | copy-start | bytes 772
  0.7 21.9 %copy-start.6 = (s32[1,128]{1,0:T(1,128)S(1)}, s32[1,128]{1,0:T(1,128)}, u32[]{:S(2)}) copy-start(s32[1,128]{1,0:T(1,128)} %param.15) | copy-start | bytes 1540
  3.0 91.4 %collective-permute-start = (bf16[16,512]{1,0:T(8,128)(2,1)S(1)}, bf16[16,512]{1,0:T(8,128)(2,1)S(1)}, u32[]{:S(2)}, u32[]{:S(2)}) collective-permute-start(bf16[16,512]{1,0:T(8,128)(2,1)S(1)} %gather_fusion), channel_id=1, source_target_pairs={{0,1},{1,2},{2,3},{3,4},{4,5},{5,6},{6,7},{7,0},{8,9},{9,10},{10,1... | collective-permute-start | bytes 49160 | tf_op jit(solution)/shard_map/ppermute | solution.py:17
  3.5 90.9 %collective-permute-start.1 = (bf16[16,512]{1,0:T(8,128)(2,1)S(1)}, bf16[16,512]{1,0:T(8,128)(2,1)S(1)}, u32[]{:S(2)}, u32[]{:S(2)}) collective-permute-start(bf16[16,512]{1,0:T(8,128)(2,1)S(1)} %gather_fusion), channel_id=1, source_target_pairs={{1,0},{2,1},{3,2},{4,3},{5,4},{6,5},{7,6},{0,7},{9,8},{10,9},{11,1... | collective-permute-start | bytes 49160 | tf_op jit(solution)/shard_map/ppermute | solution.py:20
  10.5 8.8 %all-to-all-start.4 = ((f32[4,8,2]{1,2,0:T(2,128)}), f32[4,8,2]{1,2,0:T(2,128)S(1)}, u32[]{:S(2)}, u32[]{:S(2)}) async-start(f32[4,8,2]{1,2,0:T(2,128)} %copy.22), calls=%async_computation.4 | async-start | bytes 8192 | tf_op jit(solution)/shard_map/all_to_all | solution.py:102
  19.3 7.9 %all-to-all-start = ((f32[4,8,2]{1,2,0:T(2,128)}), f32[4,8,2]{1,2,0:T(2,128)S(1)}, u32[]{:S(2)}, u32[]{:S(2)}) async-start(f32[4,8,2]{1,2,0:T(2,128)} %copy.17), calls=%async_computation | async-start | bytes 8192 | tf_op jit(solution)/shard_map/all_to_all | solution.py:109
  27.2 8.9 %all-to-all-start.5 = ((f32[4,8,2]{0,2,1:T(2,128)}), f32[4,8,2]{0,2,1:T(2,128)S(1)}, u32[]{:S(2)}, u32[]{:S(2)}) async-start(f32[4,8,2]{0,2,1:T(2,128)} %copy.23), calls=%async_computation.5 | async-start | bytes 16384 | tf_op jit(solution)/shard_map/all_to_all | solution.py:101
  36.1 54.5 %all-to-all-start.1 = ((f32[4,8,2]{0,2,1:T(2,128)}), f32[4,8,2]{0,2,1:T(2,128)S(1)}, u32[]{:S(2)}, u32[]{:S(2)}) async-start(f32[4,8,2]{0,2,1:T(2,128)} %copy.18), calls=%async_computation.1 | async-start | bytes 16384 | tf_op jit(solution)/shard_map/all_to_all | solution.py:108
  90.6 15.8 %all-to-all-start.2 = ((f32[4,8,2,512]{3,2,1,0:T(2,128)}), f32[4,8,2,512]{3,2,1,0:T(2,128)S(1)}, u32[]{:S(2)}, u32[]{:S(2)}) async-start(f32[4,8,2,512]{3,2,1,0:T(2,128)} %reshape.178), calls=%async_computation.2 | async-start | bytes 262144 | tf_op jit(solution)/shard_map/all_to_all | solution.py:95
  107.0 10.1 %all-to-all-start.3 = ((f32[4,8,2,512]{3,2,0,1:T(2,128)}), f32[4,8,2,512]{3,2,0,1:T(2,128)S(1)}, u32[]{:S(2)}, u32[]{:S(2)}) async-start(f32[4,8,2,512]{3,2,0,1:T(2,128)} %copy.20), calls=%async_computation.3 | async-start | bytes 262144 | tf_op jit(solution)/shard_map/all_to_all | solution.py:94
where the time goes:
time: 119 us; the launch traced here: 118 us
  blocking collectives  40.5 us (34%)
  other arithmetic  25.5 us (21%)
  starting transfers between devices  25.4 us (21%)
  waiting for transfers between devices  16.3 us (14%)
  local copies, waits for them, and re-layouts  6.49 us (5%)
  matrix products  3.31 us (3%)
    all_gather x1, blocking collectives, on_device(): hub_table = lax.all_gather(hub_feats, ('role', 'dom'), axis=0, tiled=True)  40.5 us
    scatter-add x1, other arithmetic, add_block(): node_sums.at[block_targets].add(picked)  11.6 us
    scatter-add x1, other arithmetic, add_block(): node_degree.at[block_targets].add(1.0)  7.61 us
    all_to_all x1, waiting for transfers between devices, on_device(): lax.all_to_all(lax.all_to_all(outgoing[0], 'role', split_axis=0, concat_a...  5.94 us
    all_to_all x1, waiting for transfers between devices, on_device(): lax.all_to_all(lax.all_to_all(outgoing[1], 'role', split_axis=0, concat_a...  4.84 us
    all_to_all x1, starting transfers between devices, on_device(): lax.all_to_all(outgoing[1], 'role', split_axis=0, concat_axis=0, tiled=True)  4.15 us
    ppermute x1, starting transfers between devices, extended(): lax.ppermute(lax.slice_in_dim(block, 0, width, axis=dim), axis, backward)  4.09 us
    all_to_all x1, waiting for transfers between devices, on_device(): lax.all_to_all(outgoing[2], 'role', split_axis=0, concat_axis=0, tiled=True)  3.94 us
  transfers between devices with their start and end apart: 8, of which 4 were waited for; matrix products, arithmetic and copies ran while one was open for 26% of the time, Pallas kernels for 0%

commit v1 on v0

v1 whole, which is shorter than its diff:
```python
import functools

import jax
import jax.numpy as jnp
from jax import lax
from jax.experimental import pallas as pl
from jax.experimental.pallas import tpu as pltpu
from jax.sharding import PartitionSpec as P

epsilon = 1e-06
MESH = pl.DeviceIdType.MESH
F32 = jnp.float32
BF16 = jnp.bfloat16
LANES = 128


def dot(a, b):
    return lax.dot_general(a, b, (((1,), (0,)), ((), ())), preferred_element_type=F32)


def dot_t(a, b):
    return lax.dot_general(a, b, (((1,), (1,)), ((), ())), preferred_element_type=F32)


def rows_equal(count, row):
    ids = lax.broadcasted_iota(jnp.int32, (count, row.shape[1]), 0)
    return jnp.where(ids == row, 1.0, 0.0).astype(BF16)


def split(counts):
    high = jnp.floor(counts * (1.0 / 256.0)) * 256.0
    return (counts - high).astype(BF16), high.astype(BF16)


def weighted(counts, table, most):
    if most <= 256:
        return dot(counts.astype(BF16), table)
    low, high = split(counts)
    return dot(low, table) + dot(high, table)


def normalised(linear):
    rectified = jnp.maximum(linear, 0.0)
    scale = lax.rsqrt(jnp.mean(rectified * rectified, axis=1, keepdims=True) + epsilon)
    return (rectified * scale).astype(BF16)


def kernel(
    roles,
    doms,
    node_ref,
    hub_ref,
    weight_hbm,
    edge_src_ref,
    edge_dst_ref,
    bound_ref,
    hub_src_ref,
    hub_slot_ref,
    slot_hub_ref,
    node_out_ref,
    hub_out_ref,
    weight_ref,
    table,
    exports,
    bounds,
    part_out,
    part_in,
    owner_out,
    owner_in,
    weight_sem,
    bound_send,
    bound_recv,
    hub_send_dom,
    hub_recv_dom,
    hub_send_role,
    hub_recv_role,
    part_send,
    part_recv,
    owner_send,
    owner_recv,
):
    r = lax.axis_index("role")
    d = lax.axis_index("dom")
    barrier = pltpu.get_barrier_semaphore()
    for o in range(1, doms):
        pl.semaphore_signal(barrier, inc=1, device_id=(r, (d + o) % doms), device_id_type=MESH)
    for o in range(1, roles):
        pl.semaphore_signal(barrier, inc=1, device_id=((r + o) % roles, d), device_id_type=MESH)
    weight_copy = pltpu.make_async_copy(weight_hbm, weight_ref, weight_sem)
    weight_copy.start()

    nodes, width = node_ref.shape
    hub_local = hub_ref.shape[0]
    devices = roles * doms
    hubs = devices * hub_local
    bound = bound_ref.shape[1]
    edges = edge_src_ref.shape[1]
    hub_edges = hub_src_ref.shape[1]
    slots = slot_hub_ref.shape[1]
    per_owner = slots // devices
    node = node_ref[...]

    def copy(src, dst, send, recv, to_role, to_dom):
        return pltpu.make_async_remote_copy(
            src_ref=src, dst_ref=dst, send_sem=send, recv_sem=recv,
            device_id=(to_role, to_dom), device_id_type=MESH,
        )

    table[r, d] = hub_ref[...]
    eye = lax.broadcasted_iota(jnp.int32, (bound, bound), 0) == lax.broadcasted_iota(
        jnp.int32, (bound, bound), 1
    )
    column = jnp.sum(jnp.where(eye, bound_ref[...].astype(F32), 0.0), axis=1, keepdims=True)
    lane = lax.broadcasted_iota(jnp.int32, (bound, nodes), 1).astype(F32)
    pick = jnp.where(lane == column, 1.0, 0.0).astype(BF16)
    exports[...] = dot(pick, node).astype(BF16)

    slot = hub_slot_ref[...]
    slot_onehot = rows_equal(slots, slot)
    slot_hubs = jnp.broadcast_to(slot_hub_ref[...].astype(F32), (8, slots)).astype(BF16)
    hub_number = dot(slot_hubs, slot_onehot)[0:1, :].astype(jnp.int32)
    owner_onehot = rows_equal(hubs, (slot // per_owner) * hub_local + hub_number)
    hub_counts = dot_t(owner_onehot, rows_equal(nodes, hub_src_ref[...]))
    hub_part = weighted(hub_counts, node, hub_edges)
    degree = jnp.sum(hub_counts, axis=1, keepdims=True)
    degree_high = jnp.floor(degree * (1.0 / 256.0)) * 256.0
    lanes = lax.broadcasted_iota(jnp.int32, (hubs, LANES), 1)
    extra = jnp.where(lanes == 0, degree - degree_high, jnp.where(lanes == 1, degree_high, 0.0))
    group = doms * hub_local
    part_out[:, :, 0:width] = hub_part.astype(BF16).reshape(roles, group, width)
    part_out[:, :, width:] = extra.astype(BF16).reshape(roles, group, LANES)

    pl.semaphore_wait(barrier, doms - 1 + roles - 1)

    hub_dom = []
    for o in range(1, doms):
        c = copy(hub_ref, table.at[r, d], hub_send_dom.at[o - 1], hub_recv_dom.at[o - 1], r, (d + o) % doms)
        c.start()
        hub_dom.append(c)
    parts = []
    for o in range(1, roles):
        to = (r + o) % roles
        c = copy(part_out.at[to], part_in.at[o - 1], part_send.at[o - 1], part_recv.at[o - 1], to, d)
        c.start()
        parts.append(c)
    sides = []
    for side, step in ((0, 1), (1, doms - 1)):
        c = copy(exports, bounds.at[side], bound_send.at[side], bound_recv.at[side], r, (d + step) % doms)
        c.start()
        sides.append(c)

    source = edge_src_ref[...]
    target_onehot = rows_equal(nodes, edge_dst_ref[...])
    counts_local = dot_t(target_onehot, rows_equal(nodes, source))
    counts_hub = dot_t(target_onehot, rows_equal(hubs, source - (nodes + 2 * bound)))

    for o in range(1, doms):
        copy(
            hub_ref, table.at[r, (d + doms - o) % doms], hub_send_dom.at[o - 1], hub_recv_dom.at[o - 1], r, d
        ).wait_recv()
    hub_role = []
    for o in range(1, roles):
        c = copy(
            table.at[r], table.at[r], hub_send_role.at[o - 1], hub_recv_role.at[o - 1], (r + o) % roles, d
        )
        c.start()
        hub_role.append(c)

    for c in parts:
        c.wait_recv()
    owner_part = part_out[r].astype(F32)
    for o in range(1, roles):
        owner_part = owner_part + part_in[o - 1].astype(F32)
    for j in range(doms):
        owner_out[j] = owner_part[j * hub_local : (j + 1) * hub_local]
    owners = []
    counts_bound = dot_t(target_onehot, rows_equal(2 * bound, source - nodes))
    for o in range(1, doms):
        to = (d + o) % doms
        c = copy(owner_out.at[to], owner_in.at[o - 1], owner_send.at[o - 1], owner_recv.at[o - 1], r, to)
        c.start()
        owners.append(c)

    node_degree = (
        jnp.sum(counts_local, axis=1, keepdims=True)
        + jnp.sum(counts_hub, axis=1, keepdims=True)
        + jnp.sum(counts_bound, axis=1, keepdims=True)
    )
    node_sum = weighted(counts_local, node, edges)
    weight_copy.wait()
    node_linear = dot(node, weight_ref[0:width])
    hub_linear = dot(hub_ref[...], weight_ref[0:width])
    for c in sides:
        c.wait_recv()
    node_sum = node_sum + weighted(counts_bound, bounds[...].reshape(2 * bound, width), edges)

    for o in range(1, roles):
        source_role = (r + roles - o) % roles
        copy(
            table.at[r], table.at[source_role], hub_send_role.at[o - 1], hub_recv_role.at[o - 1], r, d
        ).wait_recv()
    hub_table = table[...].astype(F32).reshape(hubs, width).astype(BF16)
    node_sum = node_sum + weighted(counts_hub, hub_table, edges)
    node_mean = (node_sum / node_degree).astype(BF16)
    node_out_ref[...] = normalised(node_linear + dot(node_mean, weight_ref[width:]))

    for c in owners:
        c.wait_recv()
    owner_sum = owner_out[d]
    for o in range(1, doms):
        owner_sum = owner_sum + owner_in[o - 1]
    hub_degree = jnp.sum(owner_sum[:, width:], axis=1, keepdims=True)
    hub_mean = (owner_sum[:, 0:width] / hub_degree).astype(BF16)
    hub_out_ref[...] = normalised(hub_linear + dot(hub_mean, weight_ref[width:]))

    for c in hub_dom + parts + sides + hub_role + owners:
        c.wait_send()


def solution(mesh):
    roles, doms = mesh.shape["role"], mesh.shape["dom"]

    def on_device(node, hub, weight, *lists):
        nodes, width = node.shape
        hub_local = hub.shape[0]
        bound = lists[2].shape[1]
        vmem = pl.BlockSpec(memory_space=pltpu.VMEM)
        dma = pltpu.SemaphoreType.DMA
        return pl.pallas_call(
            functools.partial(kernel, roles, doms),
            out_shape=(
                jax.ShapeDtypeStruct(node.shape, BF16),
                jax.ShapeDtypeStruct(hub.shape, BF16),
            ),
            in_specs=[vmem, vmem, pl.BlockSpec(memory_space=pl.ANY)] + [vmem] * 6,
            out_specs=(vmem, vmem),
            scratch_shapes=[
                pltpu.VMEM(weight.shape, BF16),
                pltpu.VMEM((roles, doms, hub_local, width), BF16),
                pltpu.VMEM((bound, width), BF16),
                pltpu.VMEM((2, bound, width), BF16),
                pltpu.VMEM((roles, doms * hub_local, width + LANES), BF16),
                pltpu.VMEM((roles - 1, doms * hub_local, width + LANES), BF16),
                pltpu.VMEM((doms, hub_local, width + LANES), F32),
                pltpu.VMEM((doms - 1, hub_local, width + LANES), F32),
                dma,
                dma((2,)),
                dma((2,)),
                dma((doms - 1,)),
                dma((doms - 1,)),
                dma((roles - 1,)),
                dma((roles - 1,)),
                dma((roles - 1,)),
                dma((roles - 1,)),
                dma((doms - 1,)),
                dma((doms - 1,)),
            ],
            compiler_params=pltpu.CompilerParams(collective_id=0, has_side_effects=True),
        )(node, hub, weight, *lists)

    split_rows = P(("role", "dom"), None)
    return jax.shard_map(
        on_device,
        mesh=mesh,
        in_specs=(split_rows, split_rows, P()) + (split_rows,) * 6,
        out_specs=(split_rows, split_rows),
        check_vma=False,
    )
```

time: 119 us -> 18.2 us (0.15)
  blocking collectives: 40.5 us -> 0 us
  other arithmetic: 25.5 us -> 0 us
  starting transfers between devices: 25.4 us -> 0 us
  waiting for transfers between devices: 16.3 us -> 0 us
  Pallas kernels: 0 us -> 15.2 us
  local copies, waits for them, and re-layouts: 6.49 us -> 2.17 us
  matrix products: 3.31 us -> 0 us
    all_gather x1 -> x0, blocking collectives: 40.5 us -> none  [on_device(): hub_table = lax.all_gather(hub_feats, ('role', 'dom'), axis=0, tiled=True)]
    scatter-add x4 -> x0, other arithmetic: 22.6 us -> none  [the longest x1 11.6 us: add_block(): node_sums.at[block_targets].add(picked)]
    all_to_all x6 -> x0, starting transfers between devices: 20.8 us -> none  [the longest x1 4.15 us: on_device(): lax.all_to_all(outgoing[1], 'role', split_axis=0, concat_axis=0, tiled=True)]
    all_to_all x6 -> x0, waiting for transfers between devices: 16.3 us -> none  [the longest x1 5.94 us: on_device(): lax.all_to_all(lax.all_to_all(outgoing[0], 'role', split_axis=0, concat_a...]
    pallas_call x0 -> x1, Pallas kernels: none -> 15.2 us  [on_device(): pl.pallas_call(functools.partial(kernel, roles, doms), out_shape=(jax.Sha...]
    ppermute x2 -> x0, starting transfers between devices: 4.64 us -> none  [the longest x1 4.09 us: extended(): lax.ppermute(lax.slice_in_dim(block, 0, width, axis=dim), axis, backward)]
    dot_general x6 -> x0, matrix products: 3.31 us -> none  [the longest x2 2.19 us: sage_update(): jnp.dot(self_rows, weight[:feature_width], preferred_element_type=jnp.flo...]
    all_to_all x6 -> x0, local copies, waits for them, and re-layouts: 2.3 us -> none  [the longest x1 0.68 us: on_device(): lax.all_to_all(outgoing[1], 'role', split_axis=0, concat_axis=0, tiled=True)]
  transfers between devices with their start and end apart: 8 -> 0, of which waited for: 4 -> 0; matrix products, arithmetic and copies ran while one was open for 26% -> 0% of each run, Pallas kernels for 0% -> 0%
where the time goes in v1:
time: 18.2 us; the launch traced here: 18 us
  Pallas kernels  15.2 us (84%)
  local copies, waits for them, and re-layouts  2.17 us (12%)
  between operations  0.65 us (4%)
    pallas_call x1, Pallas kernels, on_device(): pl.pallas_call(functools.partial(kernel, roles, doms), out_shape=(jax.Sha...  15.2 us
    unnamed x4, local copies, waits for them, and re-layouts  2.17 us

profile of v1, /device:TPU:0, one launch (start us, length us, event | category | flops | bytes accessed | tf_op | source)
XLA Modules:
  0.0 18.0 jit_solution(5817519964693949972)
XLA Ops:
  0.6 15.2 %shard_map.104 = (bf16[128,512]{1,0:T(8,128)(2,1)}, bf16[4,512]{1,0:T(4,128)(2,1)}) custom-call(bf16[128,512]{1,0:T(8,128)(2,1)} %node_ref.1, bf16[4,512]{1,0:T(4,128)(2,1)} %hub_ref.1, bf16[1024,512]{1,0:T(8,128)(2,1)} %weight_hbm.1, s32[1,1024]{1,0:T(1,128)} %edge_src_ref.1, s32[1,1024]{1,0:T(1,128)} %edge_dst_ref.1, s32[1,16]{1,0:T(1,128)} %bound_ref.1, ...), custom_call_target="tpu_custom_call" | custom-call | tf_op jit(solution)/shard_map/pallas_call | solution.py:229
  15.9 0.0 copy-start
  15.9 1.6 %copy.13 = bf16[128,512]{1,0:T(8,128)(2,1)} copy(bf16[128,512]{1,0:T(8,128)(2,1)} %get-tuple-element.4) | data formatting | bytes 262144
  17.4 0.0 copy-done
  17.4 0.6 %copy.14 = bf16[4,512]{1,0:T(4,128)(2,1)} copy(bf16[4,512]{1,0:T(4,128)(2,1)S(1)} %copy-done) | data formatting | bytes 8192
Async XLA Ops:
  15.9 1.6 %copy-start = (bf16[4,512]{1,0:T(4,128)(2,1)S(1)}, bf16[4,512]{1,0:T(4,128)(2,1)}, u32[]{:S(2)}) copy-start(bf16[4,512]{1,0:T(4,128)(2,1)} %get-tuple-element.5) | copy-start | bytes 12292

commit v2 on v1

--- a/solution.py
+++ b/solution.py
@@ -48,18 +48,22 @@
 def kernel(
     roles,
     doms,
-    node_ref,
-    hub_ref,
-    weight_hbm,
-    edge_src_ref,
-    edge_dst_ref,
-    bound_ref,
-    hub_src_ref,
-    hub_slot_ref,
-    slot_hub_ref,
+    *refs,
+):
+    inputs, refs = refs[:9], refs[9:]
+    (node_out_ref, hub_out_ref), refs = refs[:2], refs[2:]
+    held, refs = refs[:9], refs[9:]
+    body(roles, doms, inputs, held, node_out_ref, hub_out_ref, *refs)
+
+
+def body(
+    roles,
+    doms,
+    inputs,
+    held,
     node_out_ref,
     hub_out_ref,
-    weight_ref,
+    load_sems,
     table,
     exports,
     bounds,
@@ -67,7 +71,6 @@
     part_in,
     owner_out,
     owner_in,
-    weight_sem,
     bound_send,
     bound_recv,
     hub_send_dom,
@@ -86,8 +89,11 @@
         pl.semaphore_signal(barrier, inc=1, device_id=(r, (d + o) % doms), device_id_type=MESH)
     for o in range(1, roles):
         pl.semaphore_signal(barrier, inc=1, device_id=((r + o) % roles, d), device_id_type=MESH)
-    weight_copy = pltpu.make_async_copy(weight_hbm, weight_ref, weight_sem)
-    weight_copy.start()
+    loads = [pltpu.make_async_copy(inputs[i], held[i], load_sems.at[i]) for i in range(9)]
+    for i in (7, 8, 6, 0, 5, 1, 3, 4, 2):
+        loads[i].start()
+    node_ref, hub_ref, weight_ref, edge_src_ref, edge_dst_ref = held[:5]
+    bound_ref, hub_src_ref, hub_slot_ref, slot_hub_ref = held[5:]
 
     nodes, width = node_ref.shape
     hub_local = hub_ref.shape[0]
@@ -98,7 +104,6 @@
     hub_edges = hub_src_ref.shape[1]
     slots = slot_hub_ref.shape[1]
     per_owner = slots // devices
-    node = node_ref[...]
 
     def copy(src, dst, send, recv, to_role, to_dom):
         return pltpu.make_async_remote_copy(
@@ -106,6 +111,17 @@
             device_id=(to_role, to_dom), device_id_type=MESH,
         )
 
+    for i in (7, 8, 6):
+        loads[i].wait()
+    slot = hub_slot_ref[...]
+    slot_onehot = rows_equal(slots, slot)
+    slot_hubs = jnp.broadcast_to(slot_hub_ref[...].astype(F32), (8, slots)).astype(BF16)
+    hub_number = dot(slot_hubs, slot_onehot)[0:1, :].astype(jnp.int32)
+    owner_onehot = rows_equal(hubs, (slot // per_owner) * hub_local + hub_number)
+    hub_counts = dot_t(owner_onehot, rows_equal(nodes, hub_src_ref[...]))
+    for i in (0, 5, 1):
+        loads[i].wait()
+    node = node_ref[...]
     table[r, d] = hub_ref[...]
     eye = lax.broadcasted_iota(jnp.int32, (bound, bound), 0) == lax.broadcasted_iota(
         jnp.int32, (bound, bound), 1
@@ -115,12 +131,6 @@
     pick = jnp.where(lane == column, 1.0, 0.0).astype(BF16)
     exports[...] = dot(pick, node).astype(BF16)
 
-    slot = hub_slot_ref[...]
-    slot_onehot = rows_equal(slots, slot)
-    slot_hubs = jnp.broadcast_to(slot_hub_ref[...].astype(F32), (8, slots)).astype(BF16)
-    hub_number = dot(slot_hubs, slot_onehot)[0:1, :].astype(jnp.int32)
-    owner_onehot = rows_equal(hubs, (slot // per_owner) * hub_local + hub_number)
-    hub_counts = dot_t(owner_onehot, rows_equal(nodes, hub_src_ref[...]))
     hub_part = weighted(hub_counts, node, hub_edges)
     degree = jnp.sum(hub_counts, axis=1, keepdims=True)
     degree_high = jnp.floor(degree * (1.0 / 256.0)) * 256.0
@@ -149,6 +159,8 @@
         c.start()
         sides.append(c)
 
+    loads[3].wait()
+    loads[4].wait()
     source = edge_src_ref[...]
     target_onehot = rows_equal(nodes, edge_dst_ref[...])
     counts_local = dot_t(target_onehot, rows_equal(nodes, source))
@@ -187,7 +199,7 @@
         + jnp.sum(counts_bound, axis=1, keepdims=True)
     )
     node_sum = weighted(counts_local, node, edges)
-    weight_copy.wait()
+    loads[2].wait()
     node_linear = dot(node, weight_ref[0:width])
     hub_linear = dot(hub_ref[...], weight_ref[0:width])
     for c in sides:
@@ -217,6 +229,17 @@
         c.wait_send()
 
 
+def hand_over(node_ref, hub_ref, node_out_ref, hub_out_ref, sems):
+    copies = [
+        pltpu.make_async_copy(node_ref, node_out_ref, sems.at[0]),
+        pltpu.make_async_copy(hub_ref, hub_out_ref, sems.at[1]),
+    ]
+    for c in copies:
+        c.start()
+    for c in copies:
+        c.wait()
+
+
 def solution(mesh):
     roles, doms = mesh.shape["role"], mesh.shape["dom"]
 
@@ -226,16 +249,17 @@
         bound = lists[2].shape[1]
         vmem = pl.BlockSpec(memory_space=pltpu.VMEM)
         dma = pltpu.SemaphoreType.DMA
-        return pl.pallas_call(
+        rows = pl.pallas_call(
             functools.partial(kernel, roles, doms),
             out_shape=(
-                jax.ShapeDtypeStruct(node.shape, BF16),
-                jax.ShapeDtypeStruct(hub.shape, BF16),
+                pltpu.VMEM(node.shape, BF16),
+                pltpu.VMEM(hub.shape, BF16),
             ),
-            in_specs=[vmem, vmem, pl.BlockSpec(memory_space=pl.ANY)] + [vmem] * 6,
+            in_specs=[pl.BlockSpec(memory_space=pl.ANY)] * 9,
             out_specs=(vmem, vmem),
-            scratch_shapes=[
-                pltpu.VMEM(weight.shape, BF16),
+            scratch_shapes=[pltpu.VMEM(x.shape, x.dtype) for x in (node, hub, weight, *lists)]
+            + [
+                dma((9,)),
                 pltpu.VMEM((roles, doms, hub_local, width), BF16),
                 pltpu.VMEM((bound, width), BF16),
                 pltpu.VMEM((2, bound, width), BF16),
@@ -243,7 +267,6 @@
                 pltpu.VMEM((roles - 1, doms * hub_local, width + LANES), BF16),
                 pltpu.VMEM((doms, hub_local, width + LANES), F32),
                 pltpu.VMEM((doms - 1, hub_local, width + LANES), F32),
-                dma,
                 dma((2,)),
                 dma((2,)),
                 dma((doms - 1,)),
@@ -257,6 +280,7 @@
             ],
             compiler_params=pltpu.CompilerParams(collective_id=0, has_side_effects=True),
         )(node, hub, weight, *lists)
+        return tuple(rows)
 
     split_rows = P(("role", "dom"), None)
     return jax.shard_map(

time: 18.2 us -> 16.2 us (0.89)
  Pallas kernels: 15.2 us -> 14.1 us
  local copies, waits for them, and re-layouts: 2.17 us -> 1.25 us
    pallas_call x1, Pallas kernels: 15.2 us -> 14.1 us  [on_device(): pl.pallas_call(functools.partial(kernel, roles, doms), out_shape=(pltpu.V...]
    unnamed x4 -> x2, local copies, waits for them, and re-layouts: 2.17 us -> 1.25 us
where the time goes in v2:
time: 16.2 us; the launch traced here: 16 us
  Pallas kernels  14.1 us (87%)
  local copies, waits for them, and re-layouts  1.25 us (8%)
  between operations  0.64 us (4%)
    pallas_call x1, Pallas kernels, on_device(): pl.pallas_call(functools.partial(kernel, roles, doms), out_shape=(pltpu.V...  14.1 us
    unnamed x2, local copies, waits for them, and re-layouts  1.25 us

profile of v2, /device:TPU:0, one launch (start us, length us, event | category | flops | bytes accessed | tf_op | source)
XLA Modules:
  0.0 16.0 jit_solution(955341855146087268)
XLA Ops:
  0.6 14.1 %shard_map.104 = (bf16[128,512]{1,0:T(8,128)(2,1)S(1)}, bf16[4,512]{1,0:T(4,128)(2,1)S(1)}) custom-call(bf16[128,512]{1,0:T(8,128)(2,1)} %refs_0_.1, bf16[4,512]{1,0:T(4,128)(2,1)} %refs_1_.1, bf16[1024,512]{1,0:T(8,128)(2,1)} %refs_2_.1, s32[1,1024]{1,0:T(1,128)} %refs_3_.1, s32[1,1024]{1,0:T(1,128)} %refs_4_.1, s32[1,16]{1,0:T(1,128)} %refs_5_.1, ...), custom_call_target="tpu_custom_call" | custom-call | tf_op jit(solution)/shard_map/pallas_call | solution.py:252
  14.7 0.7 %copy.13 = bf16[128,512]{1,0:T(8,128)(2,1)} copy(bf16[128,512]{1,0:T(8,128)(2,1)S(1)} %get-tuple-element.2) | data formatting | bytes 262144
  15.4 0.6 %copy.14 = bf16[4,512]{1,0:T(4,128)(2,1)} copy(bf16[4,512]{1,0:T(4,128)(2,1)S(1)} %get-tuple-element.3) | data formatting | bytes 8192

commit v3 on v2

--- a/solution.py
+++ b/solution.py
@@ -280,7 +280,17 @@
             ],
             compiler_params=pltpu.CompilerParams(collective_id=0, has_side_effects=True),
         )(node, hub, weight, *lists)
-        return tuple(rows)
+        anywhere = pl.BlockSpec(memory_space=pl.ANY)
+        return pl.pallas_call(
+            hand_over,
+            out_shape=(
+                jax.ShapeDtypeStruct(node.shape, BF16),
+                jax.ShapeDtypeStruct(hub.shape, BF16),
+            ),
+            in_specs=[anywhere, anywhere],
+            out_specs=(anywhere, anywhere),
+            scratch_shapes=[dma((2,))],
+        )(*(pltpu.with_memory_space_constraint(x, pltpu.VMEM) for x in rows))
 
     split_rows = P(("role", "dom"), None)
     return jax.shard_map(

time: 16.2 us -> 15.6 us (0.963)
  local copies, waits for them, and re-layouts: 1.25 us -> 0 us
  Pallas kernels: 14.1 us -> 14.8 us
    unnamed x2 -> x0, local copies, waits for them, and re-layouts: 1.25 us -> none
    pallas_call x0 -> x1, Pallas kernels: none -> 0.68 us  [on_device(): pl.pallas_call(hand_over, out_shape=(jax.ShapeDtypeStruct(node.shape, BF1...]
where the time goes in v3:
time: 15.6 us; the launch traced here: 15.4 us
  Pallas kernels  14.8 us (95%)
  between operations  0.64 us (4%)
    pallas_call x1, Pallas kernels, on_device(): pl.pallas_call(functools.partial(kernel, roles, doms), out_shape=(pltpu.V...  14.1 us
    pallas_call x1, Pallas kernels, on_device(): pl.pallas_call(hand_over, out_shape=(jax.ShapeDtypeStruct(node.shape, BF1...  0.68 us

profile of v3, /device:TPU:0, one launch (start us, length us, event | category | flops | bytes accessed | tf_op | source)
XLA Modules:
  0.0 15.4 jit_solution(18018978033677251180)
XLA Ops:
  0.6 14.1 %shard_map.104 = (bf16[128,512]{1,0:T(8,128)(2,1)S(1)}, bf16[4,512]{1,0:T(4,128)(2,1)S(1)}) custom-call(bf16[128,512]{1,0:T(8,128)(2,1)} %refs_0_.1, bf16[4,512]{1,0:T(4,128)(2,1)} %refs_1_.1, bf16[1024,512]{1,0:T(8,128)(2,1)} %refs_2_.1, s32[1,1024]{1,0:T(1,128)} %refs_3_.1, s32[1,1024]{1,0:T(1,128)} %refs_4_.1, s32[1,16]{1,0:T(1,128)} %refs_5_.1, ...), custom_call_target="tpu_custom_call" | custom-call | tf_op jit(solution)/shard_map/pallas_call | solution.py:252
  14.7 0.7 %shard_map.105 = (bf16[128,512]{1,0:T(8,128)(2,1)}, bf16[4,512]{1,0:T(4,128)(2,1)}) custom-call(bf16[128,512]{1,0:T(8,128)(2,1)S(1)} %get-tuple-element.4.node_ref, bf16[4,512]{1,0:T(4,128)(2,1)S(1)} %get-tuple-element.5.hub_ref), custom_call_target="tpu_custom_call" | custom-call | tf_op jit(solution)/shard_map/pallas_call | solution.py:284

commit v4 on v3

--- a/solution.py
+++ b/solution.py
@@ -35,8 +35,8 @@
 def weighted(counts, table, most):
     if most <= 256:
         return dot(counts.astype(BF16), table)
-    low, high = split(counts)
-    return dot(low, table) + dot(high, table)
+    both = jnp.concatenate(split(counts), axis=1)
+    return dot(both, jnp.concatenate([table, table], axis=0))
 
 
 def normalised(linear):
@@ -129,7 +129,6 @@
     column = jnp.sum(jnp.where(eye, bound_ref[...].astype(F32), 0.0), axis=1, keepdims=True)
     lane = lax.broadcasted_iota(jnp.int32, (bound, nodes), 1).astype(F32)
     pick = jnp.where(lane == column, 1.0, 0.0).astype(BF16)
-    exports[...] = dot(pick, node).astype(BF16)
 
     hub_part = weighted(hub_counts, node, hub_edges)
     degree = jnp.sum(hub_counts, axis=1, keepdims=True)
@@ -140,6 +139,7 @@
     part_out[:, :, 0:width] = hub_part.astype(BF16).reshape(roles, group, width)
     part_out[:, :, width:] = extra.astype(BF16).reshape(roles, group, LANES)
 
+    exports[...] = dot(pick, node).astype(BF16)
     pl.semaphore_wait(barrier, doms - 1 + roles - 1)
 
     hub_dom = []

time: 15.6 us -> 15.6 us (level)
  no operation moved by 1% of the time
where the time goes in v4:
time: 15.6 us; the launch traced here: 15.4 us
  Pallas kernels  14.8 us (95%)
  between operations  0.64 us (4%)
    pallas_call x1, Pallas kernels, on_device(): pl.pallas_call(functools.partial(kernel, roles, doms), out_shape=(pltpu.V...  14.1 us
    pallas_call x1, Pallas kernels, on_device(): pl.pallas_call(hand_over, out_shape=(jax.ShapeDtypeStruct(node.shape, BF1...  0.68 us

profile of v4, /device:TPU:0, one launch (start us, length us, event | category | flops | bytes accessed | tf_op | source)
XLA Modules:
  0.0 15.4 jit_solution(11853757531736753034)
XLA Ops:
  0.6 14.1 %shard_map.104 = (bf16[128,512]{1,0:T(8,128)(2,1)S(1)}, bf16[4,512]{1,0:T(4,128)(2,1)S(1)}) custom-call(bf16[128,512]{1,0:T(8,128)(2,1)} %refs_0_.1, bf16[4,512]{1,0:T(4,128)(2,1)} %refs_1_.1, bf16[1024,512]{1,0:T(8,128)(2,1)} %refs_2_.1, s32[1,1024]{1,0:T(1,128)} %refs_3_.1, s32[1,1024]{1,0:T(1,128)} %refs_4_.1, s32[1,16]{1,0:T(1,128)} %refs_5_.1, ...), custom_call_target="tpu_custom_call" | custom-call | tf_op jit(solution)/shard_map/pallas_call | solution.py:252
  14.7 0.7 %shard_map.105 = (bf16[128,512]{1,0:T(8,128)(2,1)}, bf16[4,512]{1,0:T(4,128)(2,1)}) custom-call(bf16[128,512]{1,0:T(8,128)(2,1)S(1)} %get-tuple-element.4.node_ref, bf16[4,512]{1,0:T(4,128)(2,1)S(1)} %get-tuple-element.5.hub_ref), custom_call_target="tpu_custom_call" | custom-call | tf_op jit(solution)/shard_map/pallas_call | solution.py:284
